TPU v7x, 128 devices: a whole 4x4x4 slice. The times are simulated.
128 devices in a mesh: node: 32 (over y, x, core), rhs: 4 (over z).
Axes of the slice: x: 4, y: 4, z: 4, core: 2. Of those that a mesh axis runs over, the one named last changes fastest.
Arguments:
- right_side: float32 [64, 5, 256, 128], P('rhs', None, 'node'), may hold values from -6 to 6
- diag_tiles: bfloat16 [5, 256, 128, 128], P(None, ('node', 'rhs')), may hold values from -0.25 to 1.65
- off_tiles: bfloat16 [4, 256, 4, 128, 128], P(None, ('node', 'rhs')), may hold values from -0.125 to 0.125
- src_part: int32 [4, 256, 4], P(None, 'node'), may hold values from 0 to 31, all different within a row; in each aligned block of 8 rows (0 to 7, 8 to 15, ..., all dimensions but the last counted through in order) at most 2 rows name the same one
- src_slot: int32 [4, 256, 4], P(None, 'node'), may hold values from 0 to 7
Outputs:
- solution: float32 [64, 5, 256, 128], P('rhs', None, 'node')
Inputs may be any that keep to these rules, and one draw needn't show every extreme that they name: `src_part`: over the 8 block rows of one partition at one level, each row names 4 different partitions, and no partition is named by more than 2 rows.
All inputs are finite; a program needn't handle non-finite values.
Results may differ from a plain program's by a relative error of at most 0.006.
Values may be sent and summed in bfloat16 or wider, within the bound.
A program may use at most 64 MiB of HBM per device.

v0:
```python
import jax
import jax.numpy as jnp
from jax import lax
from jax.sharding import PartitionSpec as P


def sweeps(vectors, diag_whole, off_whole, owner, slot, peers, fetch_dense, push_dense):
    columns, levels, rows_here, block_size = vectors.shape
    linked = owner.shape[0]
    fanout = owner.shape[2]
    flat_index = (owner * rows_here + slot).reshape(linked, rows_here * fanout)
    stored = []
    previous = None
    for level_at in range(levels):
        current = vectors[:, level_at]
        if level_at > 0:
            gathered = fetch_dense(previous)
            referenced = jnp.take(gathered, flat_index[level_at - 1], axis=1)
            referenced = referenced.reshape(columns, rows_here, fanout, block_size)
            coupled = jnp.einsum(
                "cbks,bkts->cbt",
                referenced,
                off_whole[level_at - 1],
                preferred_element_type=jnp.float32,
            )
            current = current - coupled
        rounded = current.astype(jnp.bfloat16)
        previous = jnp.einsum(
            "cbs,bts->cbt", rounded, diag_whole[level_at], preferred_element_type=jnp.float32
        ).astype(jnp.bfloat16)
        stored.append(previous)
    results = [None] * levels
    upper_round = None
    for level_at in range(levels - 1, -1, -1):
        if level_at < levels - 1:
            contrib_terms = jnp.einsum(
                "cbt,bkts->cbks",
                upper_round,
                off_whole[level_at],
                preferred_element_type=jnp.float32,
            )
            contrib_terms = contrib_terms.reshape(columns, rows_here * fanout, block_size)
            spread = jnp.zeros((columns, peers * rows_here, block_size), jnp.float32)
            spread = spread.at[:, flat_index[level_at]].add(contrib_terms)
            incoming = push_dense(spread)
            back_in = (stored[level_at].astype(jnp.float32) - incoming).astype(jnp.bfloat16)
        else:
            back_in = stored[level_at]
        solution = jnp.einsum(
            "cbs,bst->cbt", back_in, diag_whole[level_at], preferred_element_type=jnp.float32
        )
        upper_round = solution.astype(jnp.bfloat16)
        results[level_at] = solution
    return jnp.stack(results, axis=1)


def on_device(right_side, diag_tiles, off_tiles, src_part, src_slot):
    partitions = lax.axis_size("node")
    diag_whole, off_whole = (
        lax.all_gather(diag_tiles, "rhs", axis=1, tiled=True),
        lax.all_gather(off_tiles, "rhs", axis=1, tiled=True),
    )
    return sweeps(
        right_side,
        diag_whole,
        off_whole,
        src_part,
        src_slot,
        partitions,
        lambda x: lax.all_gather(x, "node", axis=1, tiled=True),
        lambda x: lax.psum_scatter(x, "node", scatter_dimension=1, tiled=True),
    )


def solution(mesh):
    placed = (
        P("rhs", None, "node", None),
        P(None, ("node", "rhs"), None, None),
        P(None, ("node", "rhs"), None, None, None),
        P(None, "node", None),
        P(None, "node", None),
    )
    return jax.shard_map(
        on_device,
        mesh=mesh,
        in_specs=placed,
        out_specs=P("rhs", None, "node", None),
        check_vma=False,
    )
```

profile of v0, /device:TPU:0, one launch (start us, length us, event | category | flops | bytes accessed | tf_op | source)
XLA Modules:
  0.0 627.2 jit_solution(13265562975064454400)
XLA Ops:
  8.2 28.5 %all-gather.7.cloned.1.call-done = bf16[5,8,128,128]{3,2,1,0:T(8,128)(2,1)} async-done(((bf16[5,2,128,128]{3,2,1,0:T(8,128)(2,1)}), bf16[5,8,128,128]{3,2,1,0:T(8,128)(2,1)}) %all-gather.7.cloned.1.call-update) | async-done | bytes 1310736 | tf_op jit(solution)/shard_map/all_gather | solution.py:60
  36.6 1.9 fusion.9
  40.3 41.7 %all-gather.9.cloned.1.call-done = bf16[16,256,128]{2,0,1:T(8,128)(2,1)} async-done(((bf16[16,8,128]{2,0,1:T(8,128)(2,1)}), bf16[16,256,128]{2,0,1:T(8,128)(2,1)}) %all-gather.9.cloned.1.call-update) | async-done | bytes 1048592 | tf_op jit(solution)/shard_map/all_gather | solution.py:70
  82.0 1.8 gather_fusion
  84.0 47.6 %all-gather.11.cloned.1.call-done = bf16[4,8,4,128,128]{4,3,2,1,0:T(8,128)(2,1)} async-done(((bf16[4,2,4,128,128]{4,3,2,1,0:T(8,128)(2,1)}), bf16[4,8,4,128,128]{4,3,2,1,0:T(8,128)(2,1)}) %all-gather.11.cloned.1.call-update) | async-done | bytes 4194320 | tf_op jit(solution)/shard_map/all_gather | solution.py:61
  131.6 2.4 fusion.10
  134.2 42.7 %all-gather.13.cloned.1.call-done = bf16[16,256,128]{2,0,1:T(8,128)(2,1)} async-done(((bf16[16,8,128]{2,0,1:T(8,128)(2,1)}), bf16[16,256,128]{2,0,1:T(8,128)(2,1)}) %all-gather.13.cloned.1.call-update) | async-done | bytes 1048592 | tf_op jit(solution)/shard_map/all_gather | solution.py:70
  177.0 1.8 gather_fusion.1
  178.9 2.4 fusion.11
  181.5 41.9 %all-gather.15.cloned.1.call-done = bf16[16,256,128]{2,0,1:T(8,128)(2,1)} async-done(((bf16[16,8,128]{2,0,1:T(8,128)(2,1)}), bf16[16,256,128]{2,0,1:T(8,128)(2,1)}) %all-gather.15.cloned.1.call-update) | async-done | bytes 1048592 | tf_op jit(solution)/shard_map/all_gather | solution.py:70
  223.4 1.8 gather_fusion.2
  225.4 2.4 fusion.12
  228.1 41.8 %all-gather.17.cloned.1.call-done = bf16[16,256,128]{2,0,1:T(8,128)(2,1)} async-done(((bf16[16,8,128]{2,0,1:T(8,128)(2,1)}), bf16[16,256,128]{2,0,1:T(8,128)(2,1)}) %all-gather.17.cloned.1.call-update) | async-done | bytes 1048592 | tf_op jit(solution)/shard_map/all_gather | solution.py:70
  269.9 1.8 gather_fusion.3
  271.8 1.6 fusion.8
  273.8 2.2 fusion.18
  276.1 3.0 scatter_fusion
  279.2 1.3 copy-done.1
  280.7 78.1 %reduce-scatter.5.cloned.1.call-done = f32[16,8,128]{2,0,1:T(8,128)} async-done(((f32[16,256,128]{2,0,1:T(8,128)}), f32[16,8,128]{2,0,1:T(8,128)}) %reduce-scatter.5.cloned.1.call-update) | async-done | bytes 65552 | tf_op jit(solution)/shard_map/reduce_scatter | solution.py:71
  359.8 2.2 fusion.17
  362.1 3.0 scatter_fusion.1
  365.2 1.3 copy-done.2
  366.7 78.1 %reduce-scatter.7.cloned.1.call-done = f32[16,8,128]{2,0,1:T(8,128)} async-done(((f32[16,256,128]{2,0,1:T(8,128)}), f32[16,8,128]{2,0,1:T(8,128)}) %reduce-scatter.7.cloned.1.call-update) | async-done | bytes 65552 | tf_op jit(solution)/shard_map/reduce_scatter | solution.py:71
  444.8 1.0 fusion.20
  445.8 2.2 fusion.16
  448.1 3.0 scatter_fusion.2
  451.2 1.3 copy-done.3
  452.7 78.1 %reduce-scatter.9.cloned.1.call-done = f32[16,8,128]{2,0,1:T(8,128)} async-done(((f32[16,256,128]{2,0,1:T(8,128)}), f32[16,8,128]{2,0,1:T(8,128)}) %reduce-scatter.9.cloned.1.call-update) | async-done | bytes 65552 | tf_op jit(solution)/shard_map/reduce_scatter | solution.py:71
  531.8 2.2 fusion.15
  534.2 3.0 scatter_fusion.3
  537.2 1.3 copy-done
  538.6 78.2 %reduce-scatter.11.cloned.1.call-done = f32[16,8,128]{2,0,1:T(8,128)} async-done(((f32[16,256,128]{2,0,1:T(8,128)}), f32[16,8,128]{2,0,1:T(8,128)}) %reduce-scatter.11.cloned.1.call-update) | async-done | bytes 65552 | tf_op jit(solution)/shard_map/reduce_scatter | solution.py:71
  (81 shorter events, 11.5 us)
Async XLA Ops:
  6.5 33.8 %copy-start.7 = (f32[16,5,8,128]{3,2,1,0:T(8,128)S(1)}, f32[16,5,8,128]{3,2,1,0:T(8,128)}, u32[]{:S(2)}) copy-start(f32[16,5,8,128]{3,2,1,0:T(8,128)} %param.7) | copy-start | bytes 983044
  6.5 30.1 %all-gather.7.cloned.1.call-start = ((), (), s32[]{:S(2)}) async-start(), calls=%async_computation.4 | async-start | bytes 1638400 | tf_op jit(solution)/shard_map/all_gather | solution.py:60
  7.3 74.8 %all-gather.9.cloned.1.call-start = ((), (), s32[]{:S(2)}) async-start(), calls=%async_computation.5 | async-start | bytes 1081344 | tf_op jit(solution)/shard_map/all_gather | solution.py:70
  36.6 95.0 %copy-start.4 = (bf16[5,8,128,128]{3,2,1,0:T(8,128)(2,1)S(1)}, bf16[5,8,128,128]{3,2,1,0:T(8,128)(2,1)}, u32[]{:S(2)}) copy-start(bf16[5,8,128,128]{3,2,1,0:T(8,128)(2,1)} %all-gather.7.cloned.1.call-done) | copy-start | bytes 3932164
  38.6 93.0 %all-gather.11.cloned.1.call-start = ((), (), s32[]{:S(2)}) async-start(), calls=%async_computation.6 | async-start | bytes 5242880 | tf_op jit(solution)/shard_map/all_gather | solution.py:61
  39.3 137.6 %all-gather.13.cloned.1.call-start = ((), (), s32[]{:S(2)}) async-start(), calls=%async_computation.7 | async-start | bytes 1081344 | tf_op jit(solution)/shard_map/all_gather | solution.py:70
  134.0 89.4 %all-gather.15.cloned.1.call-start = ((), (), s32[]{:S(2)}) async-start(), calls=%async_computation.8 | async-start | bytes 1081344 | tf_op jit(solution)/shard_map/all_gather | solution.py:70
  181.3 88.6 %all-gather.17.cloned.1.call-start = ((), (), s32[]{:S(2)}) async-start(), calls=%async_computation.9 | async-start | bytes 1081344 | tf_op jit(solution)/shard_map/all_gather | solution.py:70
  227.8 131.0 %reduce-scatter.5.cloned.1.call-start = ((), (), s32[]{:S(2)}) async-start(), calls=%async_computation.10 | async-start | bytes 2162688 | tf_op jit(solution)/shard_map/reduce_scatter | solution.py:71
  279.2 1.4 copy-start.1
  280.6 164.2 %reduce-scatter.7.cloned.1.call-start = ((), (), s32[]{:S(2)}) async-start(), calls=%async_computation.11 | async-start | bytes 2162688 | tf_op jit(solution)/shard_map/reduce_scatter | solution.py:71
  365.2 1.4 copy-start.2
  366.5 164.3 %reduce-scatter.9.cloned.1.call-start = ((), (), s32[]{:S(2)}) async-start(), calls=%async_computation.12 | async-start | bytes 2162688 | tf_op jit(solution)/shard_map/reduce_scatter | solution.py:71
  445.8 2.2 copy-start.5
  451.2 1.4 copy-start.3
  452.6 164.2 %reduce-scatter.11.cloned.1.call-start = ((), (), s32[]{:S(2)}) async-start(), calls=%async_computation.13 | async-start | bytes 2162688 | tf_op jit(solution)/shard_map/reduce_scatter | solution.py:71
  531.8 2.2 copy-start.6
  537.2 1.3 copy-start
Sparse Core Ops, SparseCore 0:
  9.0 27.5 all-gather.6
  38.9 43.0 all-gather.8
  83.7 47.8 all-gather.10
  134.1 42.8 all-gather.12
  181.4 41.9 all-gather.14
  227.9 41.9 all-gather.16
  280.7 78.0 reduce-scatter.4
  366.7 78.0 reduce-scatter.6
  452.7 78.0 reduce-scatter.8
  538.7 78.0 reduce-scatter.10
where the time goes:
time: 628 us; the launch traced here: 627 us
  waiting for transfers between devices  558 us (89%)
  matrix products  23.8 us (4%)
  local copies, waits for them, and re-layouts  17.6 us (3%)
  between operations  13.7 us (2%)
  other arithmetic  13.4 us (2%)
    reduce_scatter x4, waiting for transfers between devices, on_device(): lax.psum_scatter(x, 'node', scatter_dimension=1, tiled=True)  312 us
    all_gather x4, waiting for transfers between devices, on_device(): lax.all_gather(x, 'node', axis=1, tiled=True)  168 us
    all_gather x1, waiting for transfers between devices, on_device(): lax.all_gather(off_tiles, 'rhs', axis=1, tiled=True)  47.6 us
    all_gather x1, waiting for transfers between devices, on_device(): lax.all_gather(diag_tiles, 'rhs', axis=1, tiled=True)  28.5 us
  transfers between devices with their start and end apart: 10, of which 10 were waited for; matrix products, arithmetic and copies ran while one was open for 1% of the time, Pallas kernels for 0%

commit v1 on v0

--- a/solution.py
+++ b/solution.py
@@ -60,6 +60,16 @@
         lax.all_gather(diag_tiles, "rhs", axis=1, tiled=True),
         lax.all_gather(off_tiles, "rhs", axis=1, tiled=True),
     )
+
+    def _show_forms(u, dimension_no):
+        o_now = jax.lax.all_to_all(
+            jnp.stack([u for _ in range(jax.lax.psum(1, axis_name="node"))]),
+            concat_axis=0,
+            split_axis=0,
+            axis_name="node",
+        )
+        return jnp.concatenate(o_now, axis=dimension_no)
+
     return sweeps(
         right_side,
         diag_whole,
@@ -67,7 +77,7 @@
         src_part,
         src_slot,
         partitions,
-        lambda x: lax.all_gather(x, "node", axis=1, tiled=True),
+        lambda x: _show_forms(x, 1),
         lambda x: lax.psum_scatter(x, "node", scatter_dimension=1, tiled=True),
     )
 

time: 628 us -> 522 us (0.83)
  waiting for transfers between devices: 558 us -> 429 us
  starting transfers between devices: 0.37 us -> 22.2 us
    all_gather x4 -> x0, waiting for transfers between devices: 168 us -> none  [on_device(): lax.all_gather(x, 'node', axis=1, tiled=True)]
    all_to_all x0 -> x4, waiting for transfers between devices: none -> 68.3 us  [_show_forms(): jax.lax.all_to_all(jnp.stack([u for _ in range(jax.lax.psum(1, axis_name=...]
    all_gather x1, waiting for transfers between devices: 47.6 us -> 22.1 us  [on_device(): lax.all_gather(off_tiles, 'rhs', axis=1, tiled=True)]
    all_to_all x0 -> x4, starting transfers between devices: none -> 22 us  [_show_forms(): jax.lax.all_to_all(jnp.stack([u for _ in range(jax.lax.psum(1, axis_name=...]
where the time goes in v1:
time: 522 us; the launch traced here: 521 us
  waiting for transfers between devices  429 us (82%)
  starting transfers between devices  22.2 us (4%)
  local copies, waits for them, and re-layouts  21.6 us (4%)
  matrix products  21.2 us (4%)
  between operations  13.8 us (3%)
  other arithmetic  13.4 us (3%)
    reduce_scatter x4, waiting for transfers between devices, on_device(): lax.psum_scatter(x, 'node', scatter_dimension=1, tiled=True)  310 us
    all_to_all x4, waiting for transfers between devices, _show_forms(): jax.lax.all_to_all(jnp.stack([u for _ in range(jax.lax.psum(1, axis_name=...  68.3 us
    all_gather x1, waiting for transfers between devices, on_device(): lax.all_gather(diag_tiles, 'rhs', axis=1, tiled=True)  27 us
    all_gather x1, waiting for transfers between devices, on_device(): lax.all_gather(off_tiles, 'rhs', axis=1, tiled=True)  22.1 us
    all_to_all x4, starting transfers between devices, _show_forms(): jax.lax.all_to_all(jnp.stack([u for _ in range(jax.lax.psum(1, axis_name=...  22 us
    scatter-add x4, other arithmetic, sweeps(): spread = spread.at[:, flat_index[level_at]].add(contrib_terms)  12.1 us
  transfers between devices with their start and end apart: 10, of which 10 were waited for; matrix products, arithmetic and copies ran while one was open for 1% of the time, Pallas kernels for 0%

profile of v1, /device:TPU:0, one launch (start us, length us, event | category | flops | bytes accessed | tf_op | source)
XLA Modules:
  0.0 520.8 jit_solution(10018230017432353645)
XLA Ops:
  9.6 27.0 %all-gather.3.cloned.1.call-done = bf16[5,8,128,128]{3,2,1,0:T(8,128)(2,1)} async-done(((bf16[5,2,128,128]{3,2,1,0:T(8,128)(2,1)}), bf16[5,8,128,128]{3,2,1,0:T(8,128)(2,1)}) %all-gather.3.cloned.1.call-update) | async-done | bytes 1310736 | tf_op jit(solution)/shard_map/all_gather | solution.py:60
  37.9 1.2 stack.20
  39.1 7.1 %all-to-all-start = ((bf16[32,16,8,128]{3,2,1,0:T(8,128)(2,1)}), bf16[32,16,8,128]{3,2,1,0:T(8,128)(2,1)S(1)}, u32[]{:S(2)}, u32[]{:S(2)}) async-start(bf16[32,16,8,128]{3,2,1,0:T(8,128)(2,1)} %stack.20), calls=%async_computation | async-start | bytes 2097152 | tf_op jit(solution)/shard_map/all_to_all | solution.py:65
  46.4 17.1 %all-to-all-done = bf16[32,16,8,128]{3,2,1,0:T(8,128)(2,1)S(1)} async-done(((bf16[32,16,8,128]{3,2,1,0:T(8,128)(2,1)}), bf16[32,16,8,128]{3,2,1,0:T(8,128)(2,1)S(1)}, u32[]{:S(2)}, u32[]{:S(2)}) %all-to-all-start) | async-done | bytes 1048608 | tf_op jit(solution)/shard_map/all_to_all | solution.py:65
  65.2 22.1 %all-gather.5.cloned.1.call-done = bf16[4,8,4,128,128]{4,3,2,1,0:T(8,128)(2,1)} async-done(((bf16[4,2,4,128,128]{4,3,2,1,0:T(8,128)(2,1)}), bf16[4,8,4,128,128]{4,3,2,1,0:T(8,128)(2,1)}) %all-gather.5.cloned.1.call-update) | async-done | bytes 4194320 | tf_op jit(solution)/shard_map/all_gather | solution.py:61
  87.3 1.7 fusion.10
  90.2 7.1 %all-to-all-start.1 = ((bf16[32,16,8,128]{3,2,1,0:T(8,128)(2,1)}), bf16[32,16,8,128]{3,2,1,0:T(8,128)(2,1)S(1)}, u32[]{:S(2)}, u32[]{:S(2)}) async-start(bf16[32,16,8,128]{3,2,1,0:T(8,128)(2,1)} %stack.21), calls=%async_computation.1 | async-start | bytes 2097152 | tf_op jit(solution)/shard_map/all_to_all | solution.py:65
  97.5 17.1 %all-to-all-done.1 = bf16[32,16,8,128]{3,2,1,0:T(8,128)(2,1)S(1)} async-done(((bf16[32,16,8,128]{3,2,1,0:T(8,128)(2,1)}), bf16[32,16,8,128]{3,2,1,0:T(8,128)(2,1)S(1)}, u32[]{:S(2)}, u32[]{:S(2)}) %all-to-all-start.1) | async-done | bytes 1048608 | tf_op jit(solution)/shard_map/all_to_all | solution.py:65
  116.3 1.7 fusion.11
  118.1 1.2 stack.22
  119.3 3.9 all-to-all-start.2
  123.5 17.1 %all-to-all-done.2 = bf16[32,16,8,128]{3,2,1,0:T(8,128)(2,1)S(1)} async-done(((bf16[32,16,8,128]{3,2,1,0:T(8,128)(2,1)}), bf16[32,16,8,128]{3,2,1,0:T(8,128)(2,1)S(1)}, u32[]{:S(2)}, u32[]{:S(2)}) %all-to-all-start.2) | async-done | bytes 1048608 | tf_op jit(solution)/shard_map/all_to_all | solution.py:65
  142.3 1.7 fusion.12
  145.3 3.9 all-to-all-start.3
  149.5 17.0 %all-to-all-done.3 = bf16[32,16,8,128]{3,2,1,0:T(8,128)(2,1)S(1)} async-done(((bf16[32,16,8,128]{3,2,1,0:T(8,128)(2,1)}), bf16[32,16,8,128]{3,2,1,0:T(8,128)(2,1)S(1)}, u32[]{:S(2)}, u32[]{:S(2)}) %all-to-all-start.3) | async-done | bytes 1048608 | tf_op jit(solution)/shard_map/all_to_all | solution.py:65
  168.2 1.6 fusion.8
  170.2 2.2 fusion.18
  172.5 3.0 scatter_fusion
  175.5 1.3 copy-done.1
  177.0 75.4 %reduce-scatter.5.cloned.1.call-done = f32[16,8,128]{2,0,1:T(8,128)} async-done(((f32[16,256,128]{2,0,1:T(8,128)}), f32[16,8,128]{2,0,1:T(8,128)}) %reduce-scatter.5.cloned.1.call-update) | async-done | bytes 65552 | tf_op jit(solution)/shard_map/reduce_scatter | solution.py:81
  253.4 2.2 fusion.17
  255.7 3.0 scatter_fusion.1
  258.8 1.3 copy-done.2
  260.3 78.1 %reduce-scatter.7.cloned.1.call-done = f32[16,8,128]{2,0,1:T(8,128)} async-done(((f32[16,256,128]{2,0,1:T(8,128)}), f32[16,8,128]{2,0,1:T(8,128)}) %reduce-scatter.7.cloned.1.call-update) | async-done | bytes 65552 | tf_op jit(solution)/shard_map/reduce_scatter | solution.py:81
  339.4 2.2 fusion.16
  341.7 3.0 scatter_fusion.2
  344.8 1.3 copy-done.3
  346.3 78.0 %reduce-scatter.9.cloned.1.call-done = f32[16,8,128]{2,0,1:T(8,128)} async-done(((f32[16,256,128]{2,0,1:T(8,128)}), f32[16,8,128]{2,0,1:T(8,128)}) %reduce-scatter.9.cloned.1.call-update) | async-done | bytes 65552 | tf_op jit(solution)/shard_map/reduce_scatter | solution.py:81
  425.4 2.2 fusion.15
  427.7 3.0 scatter_fusion.3
  430.8 1.3 copy-done
  432.1 78.3 %reduce-scatter.11.cloned.1.call-done = f32[16,8,128]{2,0,1:T(8,128)} async-done(((f32[16,256,128]{2,0,1:T(8,128)}), f32[16,8,128]{2,0,1:T(8,128)}) %reduce-scatter.11.cloned.1.call-update) | async-done | bytes 65552 | tf_op jit(solution)/shard_map/reduce_scatter | solution.py:81
  (101 shorter events, 22.2 us)
Async XLA Ops:
  6.5 30.1 %all-gather.3.cloned.1.call-start = ((), (), s32[]{:S(2)}) async-start(), calls=%async_computation.8 | async-start | bytes 1638400 | tf_op jit(solution)/shard_map/all_gather | solution.py:60
  7.3 80.0 %all-gather.5.cloned.1.call-start = ((), (), s32[]{:S(2)}) async-start(), calls=%async_computation.9 | async-start | bytes 5242880 | tf_op jit(solution)/shard_map/all_gather | solution.py:61
  8.0 38.4 %copy-start.10 = (f32[16,5,8,128]{3,2,1,0:T(8,128)S(1)}, f32[16,5,8,128]{3,2,1,0:T(8,128)}, u32[]{:S(2)}) copy-start(f32[16,5,8,128]{3,2,1,0:T(8,128)} %param.7) | copy-start | bytes 983044
  37.8 8.6 %copy-start.11 = (bf16[16,8,128]{2,0,1:T(8,128)(2,1)}, bf16[16,8,128]{2,0,1:T(8,128)(2,1)S(1)}, u32[]{:S(2)}) copy-start(bf16[16,8,128]{2,0,1:T(8,128)(2,1)S(1)} %fusion.9) | copy-start | bytes 98308
  39.1 24.4 %all-to-all-start = ((bf16[32,16,8,128]{3,2,1,0:T(8,128)(2,1)}), bf16[32,16,8,128]{3,2,1,0:T(8,128)(2,1)S(1)}, u32[]{:S(2)}, u32[]{:S(2)}) async-start(bf16[32,16,8,128]{3,2,1,0:T(8,128)(2,1)} %stack.20), calls=%async_computation | async-start | bytes 2097152 | tf_op jit(solution)/shard_map/all_to_all | solution.py:65
  46.4 40.8 %copy-start.4 = (bf16[5,8,128,128]{3,2,1,0:T(8,128)(2,1)S(1)}, bf16[5,8,128,128]{3,2,1,0:T(8,128)(2,1)}, u32[]{:S(2)}) copy-start(bf16[5,8,128,128]{3,2,1,0:T(8,128)(2,1)} %all-gather.3.cloned.1.call-done) | copy-start | bytes 3932164
  89.0 1.3 copy-start.7
  90.2 24.4 %all-to-all-start.1 = ((bf16[32,16,8,128]{3,2,1,0:T(8,128)(2,1)}), bf16[32,16,8,128]{3,2,1,0:T(8,128)(2,1)S(1)}, u32[]{:S(2)}, u32[]{:S(2)}) async-start(bf16[32,16,8,128]{3,2,1,0:T(8,128)(2,1)} %stack.21), calls=%async_computation.1 | async-start | bytes 2097152 | tf_op jit(solution)/shard_map/all_to_all | solution.py:65
  118.1 1.3 copy-start.8
  119.3 21.3 %all-to-all-start.2 = ((bf16[32,16,8,128]{3,2,1,0:T(8,128)(2,1)}), bf16[32,16,8,128]{3,2,1,0:T(8,128)(2,1)S(1)}, u32[]{:S(2)}, u32[]{:S(2)}) async-start(bf16[32,16,8,128]{3,2,1,0:T(8,128)(2,1)} %stack.22), calls=%async_computation.2 | async-start | bytes 2097152 | tf_op jit(solution)/shard_map/all_to_all | solution.py:65
  144.0 1.3 copy-start.9
  145.3 21.3 %all-to-all-start.3 = ((bf16[32,16,8,128]{3,2,1,0:T(8,128)(2,1)}), bf16[32,16,8,128]{3,2,1,0:T(8,128)(2,1)S(1)}, u32[]{:S(2)}, u32[]{:S(2)}) async-start(bf16[32,16,8,128]{3,2,1,0:T(8,128)(2,1)} %stack.23), calls=%async_computation.3 | async-start | bytes 2097152 | tf_op jit(solution)/shard_map/all_to_all | solution.py:65
  149.2 103.2 %reduce-scatter.5.cloned.1.call-start = ((), (), s32[]{:S(2)}) async-start(), calls=%async_computation.10 | async-start | bytes 2162688 | tf_op jit(solution)/shard_map/reduce_scatter | solution.py:81
  175.5 1.4 copy-start.1
  176.9 161.5 %reduce-scatter.7.cloned.1.call-start = ((), (), s32[]{:S(2)}) async-start(), calls=%async_computation.11 | async-start | bytes 2162688 | tf_op jit(solution)/shard_map/reduce_scatter | solution.py:81
  258.8 1.4 copy-start.2
  260.2 164.2 %reduce-scatter.9.cloned.1.call-start = ((), (), s32[]{:S(2)}) async-start(), calls=%async_computation.12 | async-start | bytes 2162688 | tf_op jit(solution)/shard_map/reduce_scatter | solution.py:81
  339.4 2.2 copy-start.5
  344.8 1.4 copy-start.3
  346.2 164.2 %reduce-scatter.11.cloned.1.call-start = ((), (), s32[]{:S(2)}) async-start(), calls=%async_computation.13 | async-start | bytes 2162688 | tf_op jit(solution)/shard_map/reduce_scatter | solution.py:81
  425.4 2.2 copy-start.6
  430.8 1.3 copy-start
Sparse Core Ops, SparseCore 0:
  9.0 27.5 all-gather.2
  38.3 48.8 all-gather.4
  177.0 75.3 reduce-scatter.4
  260.3 78.0 reduce-scatter.6
  346.3 78.0 reduce-scatter.8
  432.2 78.1 reduce-scatter.10
